TPU v7x, 128 devices: a whole 4x4x4 slice. The times are simulated.
128 devices in a mesh: dp: 8 (over x, core), fsdp: 16 (over z, y).
Axes of the slice: x: 4, y: 4, z: 4, core: 2. Of those that a mesh axis runs over, the one named last changes fastest.
Arguments:
- hidden_rows: bfloat16 [2048, 15360], P('fsdp', 'dp'), may hold values from -6 to 6
- upstream: bfloat16 [2048, 4096], P('fsdp'), may hold values from -6 to 6
- advantages: float32 [16, 4], P('fsdp'), may hold values from -4 to 4
- lengths: int32 [16, 4], P('fsdp'), may hold values from 1 to 64, 128 in all within a row
- dest_rank: int32 [256, 1], P('fsdp'), may hold values from 0 to 15; in each aligned block of 16 rows (0 to 15, 16 to 31, ...) at most 2 rows name the same one
- w_down: bfloat16 [15360, 4096], P('dp', 'fsdp'), may hold values from -0.046875 to 0.046875
Outputs:
- packed_out: bfloat16 [4096, 4096], P('fsdp', 'dp')
- packed_back: bfloat16 [4096, 15360], P('fsdp', 'dp')
- weight_grad: float32 [15360, 4096], P('dp', 'fsdp')
Inputs may be any that keep to these rules, and one draw needn't show every extreme that they name: Each generator group's 4 lengths sum to 128, the largest is 64. `dest_rank`: among the 16 blocks of one generator group, at most 2 name the same learner rank, and some learner is named 2 times.
All inputs are finite; a program needn't handle non-finite values.
Results may differ from a plain program's by a relative error of at most 0.014.
Values may be sent and summed in bfloat16 or wider, within the bound.
No kernel may reach another device: no remote copies, remote signals or barrier semaphores. Data moves between devices by JAX's collectives and lax.ppermute only.
A program may use at most 128 MiB of HBM per device.

v0:
```python
import jax
import jax.numpy as jnp
from jax import lax
from jax.sharding import PartitionSpec as P

SENDB = 2


def rounded(value):
    return lax.optimization_barrier(value.astype(jnp.bfloat16)).astype(jnp.float32)


def on_device(hidden_rows, upstream, advantages, lengths, dest_rank, w_down):
    groups = lax.axis_size("fsdp")
    src_rows = hidden_rows.shape[0]
    per_group = lengths.shape[1]
    blocks = dest_rank.shape[0]
    block_rows = src_rows // blocks
    ends_at = jnp.cumsum(lengths[0])
    starts = ends_at - lengths[0]
    position = jnp.arange(src_rows, dtype=jnp.int32)[:, None]
    member = (position >= starts[None, :]) & (position < ends_at[None, :])
    factor = advantages[0] * (src_rows / (per_group * lengths[0].astype(jnp.float32)))
    row_weight = jnp.sum(jnp.where(member, factor[None, :], jnp.float32(0.0)), axis=1)
    scaled = (row_weight[:, None] * upstream.astype(jnp.float32)).astype(jnp.bfloat16)
    w_full = lax.all_gather(w_down, "fsdp", axis=1, tiled=True)
    partial_value = lax.dot_general(
        hidden_rows, scaled, (((0,), (0,)), ((), ())), preferred_element_type=jnp.float32
    )
    weight_grad = lax.psum_scatter(
        rounded(partial_value).astype(jnp.bfloat16), "fsdp", scatter_dimension=1, tiled=True
    ).astype(jnp.float32) / (per_group * groups)
    target = dest_rank[:, 0]
    order = jnp.arange(blocks, dtype=jnp.int32)
    earlier = order[None, :] < order[:, None]
    same = target[:, None] == target[None, :]
    slot_index = jnp.sum((same & earlier).astype(jnp.int32), axis=1)
    target_slot = target * SENDB + slot_index
    one_hot = (target_slot[None, :] == jnp.arange(groups * SENDB, dtype=jnp.int32)[:, None]).astype(
        jnp.bfloat16
    )

    def place_blocks(values):
        pieces = values.reshape(blocks, block_rows, values.shape[1])
        placed = jnp.einsum(
            "ps,sbc->pbc", one_hot, pieces, preferred_element_type=jnp.float32
        ).astype(values.dtype)
        return placed.reshape(groups, SENDB * block_rows, values.shape[1])

    hidden_recv, scaled_recv = (
        lax.all_to_all(place_blocks(hidden_rows), "fsdp", split_axis=0, concat_axis=0, tiled=True),
        lax.all_to_all(place_blocks(scaled), "fsdp", split_axis=0, concat_axis=0, tiled=True),
    )
    hidden_flat = hidden_recv.reshape(-1, hidden_recv.shape[2])
    scaled_flat = scaled_recv.reshape(-1, scaled_recv.shape[2])
    forward_part = rounded(jnp.dot(hidden_flat, w_full, preferred_element_type=jnp.float32))
    packed_out = lax.psum_scatter(
        forward_part.astype(jnp.bfloat16), "dp", scatter_dimension=1, tiled=True
    )
    packed_back = lax.dot_general(
        scaled_flat, w_full, (((1,), (1,)), ((), ())), preferred_element_type=jnp.float32
    ).astype(jnp.bfloat16)
    return (packed_out, packed_back, weight_grad)


def solution(mesh):
    placed = (
        P("fsdp", "dp"),
        P("fsdp", None),
        P("fsdp", None),
        P("fsdp", None),
        P("fsdp", None),
        P("dp", "fsdp"),
    )
    return jax.shard_map(
        on_device,
        mesh=mesh,
        in_specs=placed,
        out_specs=(P("fsdp", "dp"), P("fsdp", "dp"), P("dp", "fsdp")),
        check_vma=False,
    )
```

profile of v0, /device:TPU:0, one launch (start us, length us, event | category | flops | bytes accessed | tf_op | source)
XLA Modules:
  0.0 309.7 jit_solution(16889025768865290448)
XLA Ops:
  7.2 0.0 copy-start
  7.2 0.0 all-gather.2.cloned.1.call-start
  7.2 0.7 all-gather.2.cloned.1.call-update
  7.9 0.0 reduce-scatter.5.cloned.1.call-start
  8.0 0.8 reduce-window.4
  8.8 0.7 fusion.11
  9.5 0.7 fusion.10
  10.1 0.1 select_reduce_fusion
  10.2 0.0 copy-done
  10.2 9.4 %convert_bitcast_fusion = bf16[1920,4096]{0,1:T(8,128)(2,1)} fusion(bf16[128,1920]{1,0:T(8,128)(2,1)S(1)} %copy-done, bf16[128,4096]{1,0:T(8,128)(2,1)} %param.7, f32[128]{0:T(128)S(1)} %select_reduce_fusion), kind=kOutput, calls=%fused_computation | convolution fusion | flops 2022703104 | bytes 17269248 | tf_op jit(solution)/shard_map/dot_general | solution.py:27
  19.6 0.0 copy-start.2
  19.6 0.0 reduce-scatter.5.cloned.1.call-update
  19.7 0.0 reduce-scatter.3.cloned.1.call-start
  19.7 0.6 copy-done.2
  20.3 0.2 convert_reduce_fusion
  20.5 0.5 convolution_convert_fusion.3
  21.0 0.3 copy.18
  21.3 29.7 %all_to_all.10 = bf16[16,16,1920]{2,1,0:T(8,128)(2,1)S(1)} all-to-all(bf16[16,16,1920]{2,1,0:T(8,128)(2,1)S(1)} %bitcast.32), channel_id=1, replica_groups=mesh['dp'=8,'fsdp'=16] {'fsdp'}, dimensions={0} | all-to-all | bytes 1966080 | tf_op jit(solution)/shard_map/all_to_all | solution.py:51
  51.0 85.3 %all-gather.2.cloned.1.call-done = bf16[1920,4096]{1,0:T(8,128)(2,1)} async-done(((bf16[1920,256]{1,0:T(8,128)(2,1)}), bf16[1920,4096]{1,0:T(8,128)(2,1)}) %all-gather.2.cloned.1.call-update) | async-done | bytes 15728656 | tf_op jit(solution)/shard_map/all_gather | solution.py:26
  136.4 11.5 %convolution_convert_fusion = bf16[256,4096]{1,0:T(8,128)(2,1)} fusion(bf16[256,1920]{1,0:T(8,128)(2,1)S(1)} %bitcast.34, bf16[1920,4096]{1,0:T(8,128)(2,1)} %all-gather.2.cloned.1.call-done), kind=kOutput, calls=%fused_computation.1 | convolution fusion | flops 4027580416 | bytes 18808832 | tf_op jit(solution)/shard_map/dot_general | solution.py:56
  147.8 0.0 copy-start.1
  147.8 0.0 reduce-scatter.3.cloned.1.call-update
  147.9 1.5 copy-done.1
  149.4 0.3 fusion.2
  149.6 1.4 convolution_convert_fusion.1
  151.1 1.2 copy.20
  152.2 50.2 %all_to_all.11 = bf16[16,16,4096]{2,1,0:T(8,128)(2,1)S(1)} all-to-all(bf16[16,16,4096]{2,1,0:T(8,128)(2,1)S(1)} %bitcast.31), channel_id=1, replica_groups=mesh['dp'=8,'fsdp'=16] {'fsdp'}, dimensions={0} | all-to-all | bytes 4194304 | tf_op jit(solution)/shard_map/all_to_all | solution.py:52
  202.4 9.7 %convolution_convert_fusion.2 = bf16[256,1920]{1,0:T(8,128)(2,1)} fusion(bf16[256,4096]{1,0:T(8,128)(2,1)S(1)} %bitcast.33, bf16[1920,4096]{1,0:T(8,128)(2,1)} %all-gather.2.cloned.1.call-done), kind=kOutput, calls=%fused_computation.3 | convolution fusion | flops 4027023360 | bytes 18808832 | tf_op jit(solution)/shard_map/dot_general | solution.py:60
  212.0 55.4 %reduce-scatter.5.cloned.1.call-done = bf16[1920,256]{0,1:T(8,128)(2,1)} async-done(((bf16[1920,4096]{0,1:T(8,128)(2,1)}), bf16[1920,256]{0,1:T(8,128)(2,1)}) %reduce-scatter.5.cloned.1.call-update) | async-done | bytes 983056 | tf_op jit(solution)/shard_map/reduce_scatter | solution.py:30
  267.5 1.3 convert_multiply_fusion
  268.8 1.8 copy.21
  270.6 32.5 %reduce-scatter.3.cloned.1.call-done = bf16[256,512]{1,0:T(8,128)(2,1)} async-done(((bf16[256,4096]{1,0:T(8,128)(2,1)}), bf16[256,512]{1,0:T(8,128)(2,1)}) %reduce-scatter.3.cloned.1.call-update) | async-done | bytes 262160 | tf_op jit(solution)/shard_map/reduce_scatter | solution.py:57
  (1 shorter events, 0.0 us)
Async XLA Ops:
  7.2 3.1 copy-start
  7.2 129.2 %all-gather.2.cloned.1.call-start = ((), (), s32[]{:S(2)}) async-start(), calls=%async_computation.4 | async-start | bytes 16711680 | tf_op jit(solution)/shard_map/all_gather | solution.py:26
  7.9 259.6 %reduce-scatter.5.cloned.1.call-start = ((), (), s32[]{:S(2)}) async-start(), calls=%async_computation.6 | async-start | bytes 16711680 | tf_op jit(solution)/shard_map/reduce_scatter | solution.py:30
  19.6 0.7 copy-start.2
  19.7 283.5 %reduce-scatter.3.cloned.1.call-start = ((), (), s32[]{:S(2)}) async-start(), calls=%async_computation.5 | async-start | bytes 2359296 | tf_op jit(solution)/shard_map/reduce_scatter | solution.py:57
  147.8 1.5 copy-start.1
Sparse Core Ops, SparseCore 0:
  10.1 126.2 all-gather.1
  139.8 127.6 reduce-scatter.4
  270.5 32.6 reduce-scatter.2
where the time goes:
time: 310 us
  waiting for transfers between devices  174 us (56%)
  blocking collectives  79.9 us (26%)
  matrix products  32.5 us (10%)
  between operations  13.8 us (4%)
  local copies, waits for them, and re-layouts  5.33 us (2%)
  other arithmetic  4.03 us (1%)
    all_gather x1, waiting for transfers between devices, on_device(): w_full = lax.all_gather(w_down, 'fsdp', axis=1, tiled=True)  85.3 us
    reduce_scatter x1, waiting for transfers between devices, on_device(): lax.psum_scatter(rounded(partial_value).astype(jnp.bfloat16), 'fsdp', sca...  55.4 us
    all_to_all x1, blocking collectives, on_device(): lax.all_to_all(place_blocks(scaled), 'fsdp', split_axis=0, concat_axis=0,...  50.2 us
    reduce_scatter x1, waiting for transfers between devices, on_device(): lax.psum_scatter(forward_part.astype(jnp.bfloat16), 'dp', scatter_dimensi...  32.5 us
    all_to_all x1, blocking collectives, on_device(): lax.all_to_all(place_blocks(hidden_rows), 'fsdp', split_axis=0, concat_ax...  29.7 us
    dot_general x1, matrix products, on_device(): jnp.dot(hidden_flat, w_full, preferred_element_type=jnp.float32)  11.5 us
    dot_general x1, matrix products, on_device(): lax.dot_general(scaled_flat, w_full, (((1,), (1,)), ((), ())), preferred_...  9.67 us
    dot_general x1, matrix products, on_device(): lax.dot_general(hidden_rows, scaled, (((0,), (0,)), ((), ())), preferred_...  9.42 us
  transfers between devices with their start and end apart: 3, of which 3 were waited for; matrix products, arithmetic and copies ran while one was open for 13% of the time, Pallas kernels for 0%

commit v1 on v0

v1 whole, which is shorter than its diff:
```python
import jax
import jax.numpy as jnp
from jax import lax
from jax.experimental import pallas as pl
from jax.experimental.pallas import tpu as pltpu
from jax.sharding import PartitionSpec as P

SENDB = 2
F32, BF16 = jnp.float32, jnp.bfloat16
AXES = ("dp", "fsdp")


def pairs_of(move):
    at = lambda x, c, z, y: (2 * x + c) * 16 + 4 * z + y
    return [
        (at(x, c, z, y), at(*move(x, c, z, y)))
        for x in range(4) for c in range(2) for z in range(4) for y in range(4)
    ]


def along_a(step):
    return pairs_of(lambda x, c, z, y: (x, c, z, (y + step) % 4) if c else (x, c, (z + step) % 4, y))


def along_b(step):
    return pairs_of(lambda x, c, z, y: (x, c, (z + step) % 4, y) if c else (x, c, z, (y + step) % 4))


def send(value, pairs):
    return lax.ppermute(value, AXES, pairs)


def together(*values):
    return lax.optimization_barrier(values)


def scale_rows(place, advantages, lengths, upstream):
    rows = upstream.shape[0]
    width = upstream.shape[1] // 16

    def body(place_ref, adv_ref, len_ref, up_ref, *outs):
        row = lax.broadcasted_iota(jnp.int32, (rows, width), 0)
        weight = jnp.zeros((rows, width), F32)
        start = jnp.int32(0)
        for k in range(4):
            size = len_ref[0, k]
            inside = (row >= start) & (row < start + size)
            sized = jnp.full((rows, width), size, jnp.int32).astype(F32)
            weight = jnp.where(inside, adv_ref[0, k] * (rows / (4 * sized)), weight)
            start = start + size
        c, a, b = place_ref[1], place_ref[2], place_ref[3]
        for q in range(4):
            for p in range(4):
                far, near = (a + q) % 4, (b + p) % 4
                block = jnp.where(c == 0, 4 * far + near, 4 * near + far)
                part = up_ref[:, pl.ds(pl.multiple_of(block * width, width), width)]
                outs[q][:, p * width:(p + 1) * width] = (weight * part.astype(F32)).astype(BF16)

    smem = pl.BlockSpec(memory_space=pltpu.SMEM)
    vmem = pl.BlockSpec(memory_space=pltpu.VMEM)
    return pl.pallas_call(
        body,
        out_shape=[jax.ShapeDtypeStruct((rows, 4 * width), BF16)] * 4,
        in_specs=[smem, smem, smem, vmem],
        out_specs=[vmem] * 4,
        compiler_params=pltpu.CompilerParams(vmem_limit_bytes=8 << 20),
        name="scale_rows",
    )(place, advantages, lengths, upstream)


SMEM = pl.BlockSpec(memory_space=pltpu.SMEM)
VMEM = pl.BlockSpec(memory_space=pltpu.VMEM)


def shaped(*shape):
    return jax.ShapeDtypeStruct(shape, BF16)


def limit(mib):
    return pltpu.CompilerParams(vmem_limit_bytes=mib << 20)


TILE = 384


def stacked(refs, dim):
    return jnp.concatenate([ref[...] for ref in refs], dim)


def row_blocks(pieces, block, at):
    return [pl.BlockSpec((piece.shape[0], block), at) for piece in pieces]


def back_rows(scaled, weights):
    rows, feats = scaled[0].shape
    hid = weights[0].shape[0]
    n_w = len(weights)

    def body(*refs):
        s, w, outs, full = refs[:4], refs[4:4 + n_w], refs[4 + n_w:8 + n_w], refs[8 + n_w]

        @pl.when(pl.program_id(0) == 0)
        def _():
            for i in range(4):
                full[i * rows:(i + 1) * rows, :] = s[i][...]

        total = lax.dot_general(full[...], stacked(w, 1), (((1,), (1,)), ((), ())), preferred_element_type=F32)
        for i in range(4):
            outs[i][...] = total[i * rows:(i + 1) * rows].astype(BF16)

    return pl.pallas_call(
        body,
        grid=(hid // TILE,),
        out_shape=[shaped(rows, hid)] * 4,
        in_specs=[pl.BlockSpec((rows, feats), lambda n: (0, 0))] * 4
        + [pl.BlockSpec((TILE, w.shape[1]), lambda n: (n, 0)) for w in weights],
        out_specs=[pl.BlockSpec((rows, TILE), lambda n: (0, n))] * 4,
        scratch_shapes=[pltpu.VMEM((4 * rows, feats), BF16)],
        compiler_params=limit(16),
        name="back_rows",
    )(*scaled, *weights)


def weight_parts(hidden, scaled):
    rows, feats = scaled[0].shape
    hid = hidden[0].shape[1]
    width = feats // 4
    n_h = len(hidden)

    def body(*refs):
        h, s, outs, full = refs[:n_h], refs[n_h:n_h + 4], refs[n_h + 4:n_h + 8], refs[n_h + 8]

        @pl.when(pl.program_id(0) == 0)
        def _():
            for i in range(4):
                full[i * rows:(i + 1) * rows, :] = s[i][...]

        left = stacked(h, 0)
        for p in range(4):
            outs[p][...] = lax.dot_general(
                left, full[:, p * width:(p + 1) * width], (((0,), (0,)), ((), ())), preferred_element_type=F32).astype(BF16)

    return pl.pallas_call(
        body,
        grid=(hid // TILE,),
        out_shape=[shaped(hid, width)] * 4,
        in_specs=row_blocks(hidden, TILE, lambda n: (0, n)) + [pl.BlockSpec((rows, feats), lambda n: (0, 0))] * 4,
        out_specs=[pl.BlockSpec((TILE, width), lambda n: (n, 0))] * 4,
        scratch_shapes=[pltpu.VMEM((4 * rows, feats), BF16)],
        compiler_params=limit(16),
        name="weight_parts",
    )(*hidden, *scaled)


def out_parts(place, hidden, weights):
    hid = hidden[0].shape[1]
    rows = 128
    width = 256
    n_h, n_w = len(hidden), len(weights)

    def body(place_ref, *refs):
        h, w, outs = refs[:n_h], refs[n_h:n_h + n_w], refs[n_h + n_w:n_h + n_w + 4]
        left, total = refs[n_h + n_w + 4:]
        step = pl.program_id(0)

        @pl.when(step == 0)
        def _():
            start = 0
            for ref in h:
                left[start:start + ref.shape[0], :] = ref[...]
                start += ref.shape[0]

        part = jnp.dot(left[pl.ds(pl.multiple_of(step * rows, rows), rows), :], stacked(w, 1), preferred_element_type=F32).astype(BF16)
        for p in range(4):
            total[p, step] = part[:, p * width:(p + 1) * width]

        @pl.when(step == 3)
        def _():
            x, c, a, b = place_ref[0], place_ref[1], place_ref[2], place_ref[3]
            for k in range(4):
                group, block = (a - x - k + 8) % 4, (x + k - b + 8) % 4
                for u in range(4):
                    i = jnp.where(c == 0, group, u)
                    p = jnp.where(c == 0, u, block)
                    outs[k][u] = total[p, i]

    whole = lambda v: pl.BlockSpec(v.shape, lambda n: (0, 0), pipeline_mode=pl.Buffered(1))
    return pl.pallas_call(
        body,
        grid=(4,),
        out_shape=[shaped(4, rows, width)] * 4,
        in_specs=[SMEM] + [whole(v) for v in hidden] + [whole(w) for w in weights],
        out_specs=[pl.BlockSpec((4, rows, width), lambda n: (0, 0, 0))] * 4,
        scratch_shapes=[pltpu.VMEM((4 * rows, hid), BF16), pltpu.VMEM((4, 4, rows, width), BF16)],
        compiler_params=limit(24),
        name="out_parts",
    )(place, *hidden, *weights)


def out_turn(place, own, got):
    _, rows, width = own.shape

    def body(place_ref, own_ref, g1, g2, g3, t0, t1, t2, t3):
        c, y = place_ref[1], place_ref[4]

        def total(u):
            return (own_ref[u].astype(F32) + g1[u].astype(F32) + g2[u].astype(F32) + g3[u].astype(F32)).astype(BF16)

        for j, out in enumerate((t0, t1, t2, t3)):
            half = 1 - ((y + j) % 4) // 2
            if j % 2:
                out[...] = total(j)
            else:
                out[:, :width] = total(jnp.where(c == 0, (2 * half - y + 4) % 4, j))
                out[:, width:] = total((2 * half + 1 - y + 4) % 4)

    return pl.pallas_call(
        body,
        out_shape=[shaped(rows, 2 * width), shaped(rows, width), shaped(rows, 2 * width), shaped(rows, width)],
        in_specs=[SMEM] + [VMEM] * 4,
        out_specs=[VMEM] * 4,
        compiler_params=limit(8),
        name="out_turn",
    )(place, own, *got)


def lay_rows(place, spread, turned, own, got):
    _, hid = own.shape
    width = turned[1].shape[1]

    def body(place_ref, spread_ref, t0, t1, t2, t3, b0, b1, b2, b3, out_ref):
        c, y = place_ref[1], place_ref[4]
        near = jnp.where(1 - y // 2 == c, t0[...].astype(F32), t2[...].astype(F32))
        sides = []
        for h in range(2):
            j = (2 * c + h - y + 4) % 4
            side = t0[:, :width].astype(F32)
            for n, ref in ((1, t1), (2, t2), (3, t3)):
                side = jnp.where(j == n, ref[:, :width].astype(F32), side)
            sides.append((near[:, h * width:(h + 1) * width] + side).astype(BF16))
        lay = spread_ref[...]
        out_ref[:, :2 * width] = jnp.dot(lay, jnp.concatenate(sides, 1), preferred_element_type=F32).astype(BF16)
        back = (b0[...].astype(F32) + b1[...].astype(F32) + b2[...].astype(F32) + b3[...].astype(F32)).astype(BF16)
        out_ref[:, 2 * width:] = jnp.dot(lay, back, preferred_element_type=F32).astype(BF16)

    slots = spread.shape[0]
    return pl.pallas_call(
        body,
        out_shape=shaped(slots, 2 * width + hid),
        in_specs=[SMEM] + [VMEM] * 9,
        out_specs=VMEM,
        compiler_params=limit(16),
        name="lay_rows",
    )(place, spread, *turned, own, *got)


def layer(hidden, upstream, advantages, lengths, dest_rank, w_down):
    d, f = lax.axis_index("dp"), lax.axis_index("fsdp")
    x, c, z, y = d // 2, d % 2, f // 4, f % 4
    a, b = jnp.where(c == 0, z, y), jnp.where(c == 0, y, z)
    place = jnp.stack([x, c, a, b, y]).astype(jnp.int32)

    target = dest_rank[:, 0]
    order = jnp.arange(16, dtype=jnp.int32)
    same = target[:, None] == target[None, :]
    slot = jnp.sum((same & (order[None, :] < order[:, None])).astype(jnp.int32), axis=1)
    at = ((target * SENDB + slot) * 8)[:, None] + jnp.arange(8, dtype=jnp.int32)[None, :]
    spread = (at.reshape(1, 128) == jnp.arange(256, dtype=jnp.int32)[:, None]).astype(BF16)

    h_1, h_3 = send(hidden, along_a(1)), send(hidden, along_a(-1))
    scaled = scale_rows(place, advantages, lengths, upstream)
    s_all = [scaled[0], send(scaled[1], along_a(1)), send(scaled[2], along_a(2)), send(scaled[3], along_a(-1))]
    w_3, w_1 = send(w_down, along_b(1)), send(w_down, along_b(-1))
    middle = hidden.shape[0] // 2
    h_top, h_low = send(h_1[:middle], along_a(1)), send(h_3[middle:], along_a(-1))
    h_all = [hidden, h_1, h_top, h_low, h_3]

    g_p = list(weight_parts(h_all, s_all))
    w_1, w_3, *g_p = together(w_1, w_3, *g_p)
    half = w_down.shape[1] // 2
    w_left, w_right = send(w_3[:, :half], along_b(1)), send(w_1[:, half:], along_b(-1))
    w_all = [w_down, w_1, w_left, w_right, w_3]
    got_g = [send(g_p[2], along_b(2)), send(g_p[1], along_b(1)), send(g_p[3], along_b(-1))]

    y_k = list(out_parts(place, h_all, w_all))
    got_y = [send(y_k[k], pairs_of(lambda x, c, z, y: ((x + k) % 4, c, z, y))) for k in (2, 1, 3)]

    *s_all, y_k[0] = together(*s_all, y_k[0])
    b_i = list(back_rows(s_all, w_all))
    got_b = [send(b_i[2], along_a(2)), send(b_i[3], along_a(1)), send(b_i[1], along_a(-1))]

    turned = []
    for j, value in enumerate(out_turn(place, y_k[0], got_y)):
        def home(x, c, z, y):
            if c:
                return x, y // 2, z, (y - j) % 4
            return z, 1 - ((y + j) % 4) // 2, x, y

        moves = pairs_of(home)
        if j % 2:
            moves = [(one, two) for one, two in moves if one // 16 % 2]
        turned.append(send(value, moves))

    laid = lay_rows(place, spread, turned, b_i[0], got_b).reshape(16, 16, -1)
    packed = lax.all_to_all(laid, "fsdp", split_axis=0, concat_axis=0, tiled=True).reshape(256, -1)
    weight_grad = (g_p[0].astype(F32) + got_g[0].astype(F32) + got_g[1].astype(F32) + got_g[2].astype(F32)) / 64
    return packed[:, :512], packed[:, 512:], weight_grad


def solution(mesh):
    placed = (
        P("fsdp", "dp"), P("fsdp", None), P("fsdp", None), P("fsdp", None), P("fsdp", None), P("dp", "fsdp"),
    )
    return jax.shard_map(
        layer, mesh=mesh, in_specs=placed,
        out_specs=(P("fsdp", "dp"), P("fsdp", "dp"), P("dp", "fsdp")), check_vma=False,
    )
```

time: 310 us -> 131 us (0.42)
  waiting for transfers between devices: 174 us -> 45.5 us
  blocking collectives: 79.9 us -> 0 us
  starting transfers between devices: 0.12 us -> 58.2 us
  matrix products: 32.5 us -> 0 us
  Pallas kernels: 0 us -> 15.8 us
  between operations: 13.8 us -> 0.84 us
    reduce_scatter x2 -> x0, waiting for transfers between devices: 88 us -> none  [the longest x1 55.4 us: on_device(): lax.psum_scatter(rounded(partial_value).astype(jnp.bfloat16), 'fsdp', sca...]
    all_gather x1 -> x0, waiting for transfers between devices: 85.3 us -> none  [on_device(): w_full = lax.all_gather(w_down, 'fsdp', axis=1, tiled=True)]
    all_to_all x2 -> x0, blocking collectives: 79.9 us -> none  [the longest x1 50.2 us: on_device(): lax.all_to_all(place_blocks(scaled), 'fsdp', split_axis=0, concat_axis=0,...]
    ppermute x0 -> x24, starting transfers between devices: none -> 43.1 us  [send(): return lax.ppermute(value, AXES, pairs)]
    ppermute x0 -> x24, waiting for transfers between devices: none -> 34.4 us  [send(): return lax.ppermute(value, AXES, pairs)]
    dot_general x5 -> x0, matrix products: 32.5 us -> none  [the longest x1 11.5 us: on_device(): jnp.dot(hidden_flat, w_full, preferred_element_type=jnp.float32)]
    pallas_call x0 -> x6, Pallas kernels: none -> 15.8 us  [the longest x1 4.32 us: weight_parts(): pl.pallas_call(body, grid=(hid // TILE,), out_shape=[shaped(hid, width)]...]
    all_to_all x0 -> x1, starting transfers between devices: none -> 15.1 us  [layer(): lax.all_to_all(laid, 'fsdp', split_axis=0, concat_axis=0, tiled=True)]
  transfers between devices with their start and end apart: 3 -> 25, of which waited for: 3 -> 12; matrix products, arithmetic and copies ran while one was open for 13% -> 3% of each run, Pallas kernels for 0% -> 9%
where the time goes in v1:
time: 131 us; the launch traced here: 129 us
  starting transfers between devices  58.2 us (44%)
  waiting for transfers between devices  45.5 us (35%)
  Pallas kernels  15.8 us (12%)
  local copies, waits for them, and re-layouts  4.56 us (3%)
  other arithmetic  3.86 us (3%)
    ppermute x24, starting transfers between devices, send(): return lax.ppermute(value, AXES, pairs)  43.1 us
    ppermute x24, waiting for transfers between devices, send(): return lax.ppermute(value, AXES, pairs)  34.4 us
    all_to_all x1, starting transfers between devices, layer(): lax.all_to_all(laid, 'fsdp', split_axis=0, concat_axis=0, tiled=True)  15.1 us
    all_to_all x1, waiting for transfers between devices, layer(): lax.all_to_all(laid, 'fsdp', split_axis=0, concat_axis=0, tiled=True)  11.1 us
    pallas_call x1, Pallas kernels, weight_parts(): pl.pallas_call(body, grid=(hid // TILE,), out_shape=[shaped(hid, width)]...  4.32 us
    pallas_call x1, Pallas kernels, back_rows(): pl.pallas_call(body, grid=(hid // TILE,), out_shape=[shaped(rows, hid)] *...  3.99 us
    pallas_call x1, Pallas kernels, out_parts(): pl.pallas_call(body, grid=(4,), out_shape=[shaped(4, rows, width)] * 4, i...  3.83 us
    div x1, other arithmetic, layer(): (g_p[0].astype(F32) + got_g[0].astype(F32) + got_g[1].astype(F32) + got_g...  3.57 us
  transfers between devices with their start and end apart: 25, of which 12 were waited for; matrix products, arithmetic and copies ran while one was open for 3% of the time, Pallas kernels for 9%

profile of v1, /device:TPU:0, one launch (start us, length us, event | category | flops | bytes accessed | tf_op | source)
XLA Modules:
  0.0 128.8 jit_solution(3229032603069196322)
XLA Ops:
  0.6 2.1 %collective-permute-start.3 = (bf16[128,1920]{1,0:T(8,128)(2,1)}, bf16[128,1920]{1,0:T(8,128)(2,1)S(1)}, u32[]{:S(2)}, u32[]{:S(2)}) collective-permute-start(bf16[128,1920]{1,0:T(8,128)(2,1)} %refs_0_.3), channel_id=1, source_target_pairs={{0,4},{1,5},{2,6},{3,7},{4,8},{5,9},{6,10},{7,11},{8,12},{9,13},{1... | collective-permute-start | bytes 1474568 | tf_op jit(solution)/shard_map/ppermute | solution.py:30
  2.7 3.0 %collective-permute-start.7 = (bf16[1920,256]{1,0:T(8,128)(2,1)}, bf16[1920,256]{1,0:T(8,128)(2,1)S(1)}, u32[]{:S(2)}, u32[]{:S(2)}) collective-permute-start(bf16[1920,256]{1,0:T(8,128)(2,1)} %refs_4_.1), channel_id=1, source_target_pairs={{0,3},{1,0},{2,1},{3,2},{4,7},{5,4},{6,5},{7,6},{8,11},{9,8},{10,9... | collective-permute-start | bytes 2949128 | tf_op jit(solution)/shard_map/ppermute | solution.py:30
  5.8 2.2 %collective-permute-start.5 = (bf16[128,1920]{1,0:T(8,128)(2,1)}, bf16[128,1920]{1,0:T(8,128)(2,1)S(1)}, u32[]{:S(2)}, u32[]{:S(2)}) collective-permute-start(bf16[128,1920]{1,0:T(8,128)(2,1)} %refs_0_.3), channel_id=1, source_target_pairs={{0,12},{1,13},{2,14},{3,15},{4,0},{5,1},{6,2},{7,3},{8,4},{9,5},{1... | collective-permute-start | bytes 1474568 | tf_op jit(solution)/shard_map/ppermute | solution.py:30
  8.0 0.1 stack.23.place_ref
  8.0 1.2 copy-done.2
  9.3 0.7 copy-done.5
  9.9 0.7 copy-done.6
  10.6 0.8 scale_rows.1
  11.4 2.6 %collective-permute-done.3.refs_1_ = bf16[128,1920]{1,0:T(8,128)(2,1)S(1)} collective-permute-done((bf16[128,1920]{1,0:T(8,128)(2,1)}, bf16[128,1920]{1,0:T(8,128)(2,1)S(1)}, u32[]{:S(2)}, u32[]{:S(2)}) %collective-permute-start.3) | collective-permute-done | bytes 491552 | tf_op jit(solution)/shard_map/ppermute | solution.py:30
  14.0 4.8 %collective-permute-start.1 = (bf16[128,1024]{1,0:T(8,128)(2,1)S(1)}, bf16[128,1024]{1,0:T(8,128)(2,1)S(1)}, u32[]{:S(2)}, u32[]{:S(2)}) collective-permute-start(bf16[128,1024]{1,0:T(8,128)(2,1)S(1)} %get-tuple-element.36), channel_id=1, source_target_pairs={{0,8},{1,9},{2,10},{3,11},{4,12},{5,13},{6,14},{7,15},{8,0},{9,1},... | collective-permute-start | bytes 786440 | tf_op jit(solution)/shard_map/ppermute | solution.py:30
  18.8 1.2 collective-permute-done.5.refs_4_
  20.1 3.4 %collective-permute-start.2 = (bf16[128,1024]{1,0:T(8,128)(2,1)S(1)}, bf16[128,1024]{1,0:T(8,128)(2,1)S(1)}, u32[]{:S(2)}, u32[]{:S(2)}) collective-permute-start(bf16[128,1024]{1,0:T(8,128)(2,1)S(1)} %get-tuple-element.37), channel_id=1, source_target_pairs={{0,12},{1,13},{2,14},{3,15},{4,0},{5,1},{6,2},{7,3},{8,4},{9,5},{1... | collective-permute-start | bytes 786440 | tf_op jit(solution)/shard_map/ppermute | solution.py:30
  23.6 6.0 %collective-permute-done.1.refs_7_.refs_2_ = bf16[128,1024]{1,0:T(8,128)(2,1)S(1)} collective-permute-done((bf16[128,1024]{1,0:T(8,128)(2,1)S(1)}, bf16[128,1024]{1,0:T(8,128)(2,1)S(1)}, u32[]{:S(2)}, u32[]{:S(2)}) %collective-permute-start.1) | collective-permute-done | bytes 262176 | tf_op jit(solution)/shard_map/ppermute | solution.py:30
  29.6 2.0 %collective-permute-done.4.refs_2_ = bf16[64,1920]{1,0:T(8,128)(2,1)S(1)} collective-permute-done((bf16[64,1920]{1,0:T(8,128)(2,1)S(1)}, bf16[64,1920]{1,0:T(8,128)(2,1)S(1)}, u32[]{:S(2)}, u32[]{:S(2)}) %collective-permute-start.4) | collective-permute-done | bytes 245792 | tf_op jit(solution)/shard_map/ppermute | solution.py:30
  31.6 4.2 %collective-permute-done.6.refs_3_ = bf16[64,1920]{1,0:T(8,128)(2,1)S(1)} collective-permute-done((bf16[64,1920]{1,0:T(8,128)(2,1)S(1)}, bf16[64,1920]{1,0:T(8,128)(2,1)S(1)}, u32[]{:S(2)}, u32[]{:S(2)}) %collective-permute-start.6) | collective-permute-done | bytes 245792 | tf_op jit(solution)/shard_map/ppermute | solution.py:30
  35.8 4.3 %weight_parts.1 = (bf16[1920,256]{1,0:T(8,128)(2,1)S(1)}, bf16[1920,256]{1,0:T(8,128)(2,1)}, bf16[1920,256]{1,0:T(8,128)(2,1)}, bf16[1920,256]{1,0:T(8,128)(2,1)}) custom-call(bf16[128,1920]{1,0:T(8,128)(2,1)S(1)} %copy-done.1, bf16[128,1920]{1,0:T(8,128)(2,1)S(1)} %collective-permute-done.3.refs_1_, bf16[64,1920]{1,0:T(8,128)(2,1)S(1)} %collective-permute-done.4.refs_2_, ...), custom_call_target="tpu_custom_call" | custom-call | tf_op jit(solution)/shard_map/weight_parts/pallas_call | solution.py:143
  40.2 2.1 %collective-permute-start.10 = (bf16[1920,128]{1,0:T(8,128)(2,1)S(1)}, bf16[1920,128]{1,0:T(8,128)(2,1)S(1)}, u32[]{:S(2)}, u32[]{:S(2)}) collective-permute-start(bf16[1920,128]{1,0:T(8,128)(2,1)S(1)} %slice.21), channel_id=1, source_target_pairs={{0,3},{1,0},{2,1},{3,2},{4,7},{5,4},{6,5},{7,6},{8,11},{9,8},{10,9... | collective-permute-start | bytes 1474568 | tf_op jit(solution)/shard_map/ppermute | solution.py:30
  42.2 0.1 collective-permute-start.9
  42.4 6.7 %collective-permute-done.10.refs_8_.refs_7_ = bf16[1920,128]{1,0:T(8,128)(2,1)S(1)} collective-permute-done((bf16[1920,128]{1,0:T(8,128)(2,1)S(1)}, bf16[1920,128]{1,0:T(8,128)(2,1)S(1)}, u32[]{:S(2)}, u32[]{:S(2)}) %collective-permute-start.10) | collective-permute-done | bytes 491552 | tf_op jit(solution)/shard_map/ppermute | solution.py:30
  49.1 3.3 %collective-permute-done.9.refs_7_.refs_6_ = bf16[1920,128]{1,0:T(8,128)(2,1)S(1)} collective-permute-done((bf16[1920,128]{1,0:T(8,128)(2,1)S(1)}, bf16[1920,128]{1,0:T(8,128)(2,1)S(1)}, u32[]{:S(2)}, u32[]{:S(2)}) %collective-permute-start.9) | collective-permute-done | bytes 491552 | tf_op jit(solution)/shard_map/ppermute | solution.py:30
  52.4 3.8 %out_parts.1 = (bf16[4,128,256]{2,1,0:T(8,128)(2,1)S(1)}, bf16[4,128,256]{2,1,0:T(8,128)(2,1)S(1)}, bf16[4,128,256]{2,1,0:T(8,128)(2,1)S(1)}, bf16[4,128,256]{2,1,0:T(8,128)(2,1)S(1)}) custom-call(s32[5]{0:T(128)S(1)} %stack.23.place_ref, bf16[128,1920]{1,0:T(8,128)(2,1)S(1)} %copy-done.1, bf16[128,1920]{1,0:T(8,128)(2,1)S(1)} %collective-permute-done.3.refs_1_, ...), custom_call_target="tpu_custom_call" | custom-call | tf_op jit(solution)/shard_map/out_parts/pallas_call | solution.py:188
  56.2 3.1 %collective-permute-start.11 = (bf16[4,128,256]{2,1,0:T(8,128)(2,1)S(1)}, bf16[4,128,256]{2,1,0:T(8,128)(2,1)S(1)}, u32[]{:S(2)}, u32[]{:S(2)}) collective-permute-start(bf16[4,128,256]{2,1,0:T(8,128)(2,1)S(1)} %get-tuple-element.46), channel_id=1, source_target_pairs={{0,64},{1,65},{2,66},{3,67},{4,68},{5,69},{6,70},{7,71},{8,72},{9,... | collective-permute-start | bytes 786440 | tf_op jit(solution)/shard_map/ppermute | solution.py:30
  59.3 0.6 collective-permute-start.12
  59.9 2.6 %collective-permute-start.13 = (bf16[4,128,256]{2,1,0:T(8,128)(2,1)S(1)}, bf16[4,128,256]{2,1,0:T(8,128)(2,1)S(1)}, u32[]{:S(2)}, u32[]{:S(2)}) collective-permute-start(bf16[4,128,256]{2,1,0:T(8,128)(2,1)S(1)} %get-tuple-element.48), channel_id=1, source_target_pairs={{0,96},{1,97},{2,98},{3,99},{4,100},{5,101},{6,102},{7,103},{8,104... | collective-permute-start | bytes 786440 | tf_op jit(solution)/shard_map/ppermute | solution.py:30
  62.5 4.0 %back_rows.1 = (bf16[128,1920]{1,0:T(8,128)(2,1)S(1)}, bf16[128,1920]{1,0:T(8,128)(2,1)S(1)}, bf16[128,1920]{1,0:T(8,128)(2,1)S(1)}, bf16[128,1920]{1,0:T(8,128)(2,1)S(1)}) custom-call(bf16[128,1024]{1,0:T(8,128)(2,1)S(1)} %get-tuple-element.53.refs_5_.refs_0_, bf16[128,1024]{1,0:T(8,128)(2,1)S(1)} %collective-permute-done.refs_6_.refs_1_, ...), custom_call_target="tpu_custom_call" | custom-call | tf_op jit(solution)/shard_map/back_rows/pallas_call | solution.py:111
  66.5 1.0 collective-permute-start.18
  67.6 0.1 collective-permute-done.13.g3
  67.7 0.7 out_turn.1
  68.5 1.3 %collective-permute-start.15 = (bf16[128,256]{1,0:T(8,128)(2,1)S(1)}, bf16[128,256]{1,0:T(8,128)(2,1)S(1)}, u32[]{:S(2)}, u32[]{:S(2)}) collective-permute-start(bf16[128,256]{1,0:T(8,128)(2,1)S(1)} %get-tuple-element.50), channel_id=1, source_target_pairs={{16,3},{17,0},{18,17},{19,18},{20,7},{21,4},{22,21},{23,22},{24,11... | collective-permute-start | bytes 196616 | tf_op jit(solution)/shard_map/ppermute | solution.py:30
  69.8 0.7 collective-permute-start.17
  70.4 0.2 convert_reduce_fusion
  70.6 1.0 collective-permute-start.19
  71.7 2.3 %collective-permute-start.20 = (bf16[128,1920]{1,0:T(8,128)(2,1)S(1)}, bf16[128,1920]{1,0:T(8,128)(2,1)S(1)}, u32[]{:S(2)}, u32[]{:S(2)}) collective-permute-start(bf16[128,1920]{1,0:T(8,128)(2,1)S(1)} %get-tuple-element.60), channel_id=1, source_target_pairs={{0,12},{1,13},{2,14},{3,15},{4,0},{5,1},{6,2},{7,3},{8,4},{9,5},{1... | collective-permute-start | bytes 1474568 | tf_op jit(solution)/shard_map/ppermute | solution.py:30
  73.9 0.1 collective-permute-done.15.t1
  74.0 5.5 %collective-permute-start.14 = (bf16[128,512]{1,0:T(8,128)(2,1)S(1)}, bf16[128,512]{1,0:T(8,128)(2,1)S(1)}, u32[]{:S(2)}, u32[]{:S(2)}) collective-permute-start(bf16[128,512]{1,0:T(8,128)(2,1)S(1)} %get-tuple-element.49), channel_id=1, source_target_pairs={{0,16},{1,17},{2,2},{3,3},{4,48},{5,49},{6,34},{7,35},{8,80},{9,81... | collective-permute-start | bytes 393224 | tf_op jit(solution)/shard_map/ppermute | solution.py:30
  79.5 0.7 collective-permute-start.16
  80.2 0.3 collective-permute-done.14.t0
  80.5 1.2 collective-permute-start.21
  81.7 1.1 collective-permute-start.22
  82.8 4.2 %collective-permute-start.23 = (bf16[1920,256]{1,0:T(8,128)(2,1)}, bf16[1920,256]{1,0:T(8,128)(2,1)}, u32[]{:S(2)}, u32[]{:S(2)}) collective-permute-start(bf16[1920,256]{1,0:T(8,128)(2,1)} %get-tuple-element.64), channel_id=1, source_target_pairs={{0,3},{1,0},{2,1},{3,2},{4,7},{5,4},{6,5},{7,6},{8,11},{9,8},{10,9... | collective-permute-start | bytes 2949128 | tf_op jit(solution)/shard_map/ppermute | solution.py:30
  87.1 0.1 add.51
  87.2 2.2 %lay_rows.1 = bf16[256,2432]{1,0:T(8,128)(2,1)} custom-call(s32[5]{0:T(128)S(1)} %stack.23.place_ref, bf16[256,128]{1,0:T(8,128)(2,1)S(1)} %fusion.spread_ref, bf16[128,512]{1,0:T(8,128)(2,1)S(1)} %collective-permute-done.14.t0, bf16[128,256]{1,0:T(8,128)(2,1)S(1)} %collective-permute-done.15.t1, bf16[128,512]{1,0:T(8,128)(2,1)S(1)} %collective-permute-done.16.t2, ...), custom_call_target="tpu_custom_call" | custom-call | tf_op jit(solution)/shard_map/lay_rows/pallas_call | solution.py:247
  89.4 15.1 %all-to-all-start = ((bf16[16,16,2432]{2,1,0:T(8,128)(2,1)}), bf16[16,16,2432]{2,1,0:T(8,128)(2,1)S(1)}, u32[]{:S(2)}, u32[]{:S(2)}) async-start(bf16[16,16,2432]{2,1,0:T(8,128)(2,1)} %bitcast.8), calls=%async_computation | async-start | bytes 2490368 | tf_op jit(solution)/shard_map/all_to_all | solution.py:305
  104.5 7.9 %collective-permute-done.22 = bf16[1920,256]{1,0:T(8,128)(2,1)} collective-permute-done((bf16[1920,256]{1,0:T(8,128)(2,1)}, bf16[1920,256]{1,0:T(8,128)(2,1)}, u32[]{:S(2)}, u32[]{:S(2)}) %collective-permute-start.22) | collective-permute-done | bytes 983072 | tf_op jit(solution)/shard_map/ppermute | solution.py:30
  112.4 3.6 %add_multiply_fusion = f32[1920,256]{1,0:T(8,128)} fusion(bf16[1920,256]{1,0:T(8,128)(2,1)} %collective-permute-done.23, bf16[1920,256]{1,0:T(8,128)(2,1)} %collective-permute-done.22, bf16[1920,256]{1,0:T(8,128)(2,1)} %collective-permute-done.21, bf16[1920,256]{1,0:T(8,128)(2,1)S(1)} %copy-done.4), kind=kLoop, calls=%fused_computation | loop fusion | flops 3932160 | bytes 5898240 | tf_op jit(solution)/shard_map/div | solution.py:306
  116.0 11.1 %all-to-all-done = bf16[16,16,2432]{2,1,0:T(8,128)(2,1)S(1)} async-done(((bf16[16,16,2432]{2,1,0:T(8,128)(2,1)}), bf16[16,16,2432]{2,1,0:T(8,128)(2,1)S(1)}, u32[]{:S(2)}, u32[]{:S(2)}) %all-to-all-start) | async-done | bytes 1245216 | tf_op jit(solution)/shard_map/all_to_all | solution.py:305
  127.0 1.0 slice.27
  128.0 0.7 slice.26
  (37 shorter events, 0.5 us)
Async XLA Ops:
  0.6 35.2 %copy-start.1 = (bf16[128,1920]{1,0:T(8,128)(2,1)S(1)}, bf16[128,1920]{1,0:T(8,128)(2,1)}, u32[]{:S(2)}) copy-start(bf16[128,1920]{1,0:T(8,128)(2,1)} %refs_0_.3) | copy-start | bytes 1474564
  0.6 13.4 %collective-permute-start.3 = (bf16[128,1920]{1,0:T(8,128)(2,1)}, bf16[128,1920]{1,0:T(8,128)(2,1)S(1)}, u32[]{:S(2)}, u32[]{:S(2)}) collective-permute-start(bf16[128,1920]{1,0:T(8,128)(2,1)} %refs_0_.3), channel_id=1, source_target_pairs={{0,4},{1,5},{2,6},{3,7},{4,8},{5,9},{6,10},{7,11},{8,12},{9,13},{1... | collective-permute-start | bytes 1474568 | tf_op jit(solution)/shard_map/ppermute | solution.py:30
  2.7 37.4 %collective-permute-start.7 = (bf16[1920,256]{1,0:T(8,128)(2,1)}, bf16[1920,256]{1,0:T(8,128)(2,1)S(1)}, u32[]{:S(2)}, u32[]{:S(2)}) collective-permute-start(bf16[1920,256]{1,0:T(8,128)(2,1)} %refs_4_.1), channel_id=1, source_target_pairs={{0,3},{1,0},{2,1},{3,2},{4,7},{5,4},{6,5},{7,6},{8,11},{9,8},{10,9... | collective-permute-start | bytes 2949128 | tf_op jit(solution)/shard_map/ppermute | solution.py:30
  5.8 34.4 %collective-permute-start.8 = (bf16[1920,256]{1,0:T(8,128)(2,1)}, bf16[1920,256]{1,0:T(8,128)(2,1)S(1)}, u32[]{:S(2)}, u32[]{:S(2)}) collective-permute-start(bf16[1920,256]{1,0:T(8,128)(2,1)} %refs_4_.1), channel_id=1, source_target_pairs={{0,1},{1,2},{2,3},{3,0},{4,5},{5,6},{6,7},{7,4},{8,9},{9,10},{10,1... | collective-permute-start | bytes 2949128 | tf_op jit(solution)/shard_map/ppermute | solution.py:30
  5.8 14.3 %collective-permute-start.5 = (bf16[128,1920]{1,0:T(8,128)(2,1)}, bf16[128,1920]{1,0:T(8,128)(2,1)S(1)}, u32[]{:S(2)}, u32[]{:S(2)}) collective-permute-start(bf16[128,1920]{1,0:T(8,128)(2,1)} %refs_0_.3), channel_id=1, source_target_pairs={{0,12},{1,13},{2,14},{3,15},{4,0},{5,1},{6,2},{7,3},{8,4},{9,5},{1... | collective-permute-start | bytes 1474568 | tf_op jit(solution)/shard_map/ppermute | solution.py:30
  8.0 1.2 copy-start.2
  9.3 0.7 copy-start.5
  9.9 0.7 copy-start.6
  11.3 12.2 %collective-permute-start = (bf16[128,1024]{1,0:T(8,128)(2,1)S(1)}, bf16[128,1024]{1,0:T(8,128)(2,1)S(1)}, u32[]{:S(2)}, u32[]{:S(2)}) collective-permute-start(bf16[128,1024]{1,0:T(8,128)(2,1)S(1)} %get-tuple-element.35), channel_id=1, source_target_pairs={{0,4},{1,5},{2,6},{3,7},{4,8},{5,9},{6,10},{7,11},{8,12},{9,13},{1... | collective-permute-start | bytes 786440 | tf_op jit(solution)/shard_map/ppermute | solution.py:30
  14.0 15.6 %collective-permute-start.1 = (bf16[128,1024]{1,0:T(8,128)(2,1)S(1)}, bf16[128,1024]{1,0:T(8,128)(2,1)S(1)}, u32[]{:S(2)}, u32[]{:S(2)}) collective-permute-start(bf16[128,1024]{1,0:T(8,128)(2,1)S(1)} %get-tuple-element.36), channel_id=1, source_target_pairs={{0,8},{1,9},{2,10},{3,11},{4,12},{5,13},{6,14},{7,15},{8,0},{9,1},... | collective-permute-start | bytes 786440 | tf_op jit(solution)/shard_map/ppermute | solution.py:30
  20.1 9.5 %collective-permute-start.2 = (bf16[128,1024]{1,0:T(8,128)(2,1)S(1)}, bf16[128,1024]{1,0:T(8,128)(2,1)S(1)}, u32[]{:S(2)}, u32[]{:S(2)}) collective-permute-start(bf16[128,1024]{1,0:T(8,128)(2,1)S(1)} %get-tuple-element.37), channel_id=1, source_target_pairs={{0,12},{1,13},{2,14},{3,15},{4,0},{5,1},{6,2},{7,3},{8,4},{9,5},{1... | collective-permute-start | bytes 786440 | tf_op jit(solution)/shard_map/ppermute | solution.py:30
  23.5 8.1 %collective-permute-start.4 = (bf16[64,1920]{1,0:T(8,128)(2,1)S(1)}, bf16[64,1920]{1,0:T(8,128)(2,1)S(1)}, u32[]{:S(2)}, u32[]{:S(2)}) collective-permute-start(bf16[64,1920]{1,0:T(8,128)(2,1)S(1)} %slice.24), channel_id=1, source_target_pairs={{0,4},{1,5},{2,6},{3,7},{4,8},{5,9},{6,10},{7,11},{8,12},{9,13},{1... | collective-permute-start | bytes 737288 | tf_op jit(solution)/shard_map/ppermute | solution.py:30
  29.6 6.2 %collective-permute-start.6 = (bf16[64,1920]{1,0:T(8,128)(2,1)S(1)}, bf16[64,1920]{1,0:T(8,128)(2,1)S(1)}, u32[]{:S(2)}, u32[]{:S(2)}) collective-permute-start(bf16[64,1920]{1,0:T(8,128)(2,1)S(1)} %slice.25), channel_id=1, source_target_pairs={{0,12},{1,13},{2,14},{3,15},{4,0},{5,1},{6,2},{7,3},{8,4},{9,5},{1... | collective-permute-start | bytes 737288 | tf_op jit(solution)/shard_map/ppermute | solution.py:30
  35.8 16.6 %copy-start = (bf16[1920,256]{1,0:T(8,128)(2,1)S(1)}, bf16[1920,256]{1,0:T(8,128)(2,1)}, u32[]{:S(2)}) copy-start(bf16[1920,256]{1,0:T(8,128)(2,1)} %refs_4_.1) | copy-start | bytes 2949124
  40.1 9.0 %copy-start.3 = (bf16[1920,256]{1,0:T(8,128)(2,1)}, bf16[1920,256]{1,0:T(8,128)(2,1)S(1)}, u32[]{:S(2)}) copy-start(bf16[1920,256]{1,0:T(8,128)(2,1)S(1)} %get-tuple-element.61) | copy-start | bytes 2949124
  40.2 8.9 %collective-permute-start.10 = (bf16[1920,128]{1,0:T(8,128)(2,1)S(1)}, bf16[1920,128]{1,0:T(8,128)(2,1)S(1)}, u32[]{:S(2)}, u32[]{:S(2)}) collective-permute-start(bf16[1920,128]{1,0:T(8,128)(2,1)S(1)} %slice.21), channel_id=1, source_target_pairs={{0,3},{1,0},{2,1},{3,2},{4,7},{5,4},{6,5},{7,6},{8,11},{9,8},{10,9... | collective-permute-start | bytes 1474568 | tf_op jit(solution)/shard_map/ppermute | solution.py:30
  42.2 10.1 %collective-permute-start.9 = (bf16[1920,128]{1,0:T(8,128)(2,1)S(1)}, bf16[1920,128]{1,0:T(8,128)(2,1)S(1)}, u32[]{:S(2)}, u32[]{:S(2)}) collective-permute-start(bf16[1920,128]{1,0:T(8,128)(2,1)S(1)} %slice.20), channel_id=1, source_target_pairs={{0,1},{1,2},{2,3},{3,0},{4,5},{5,6},{6,7},{7,4},{8,9},{9,10},{10,1... | collective-permute-start | bytes 1474568 | tf_op jit(solution)/shard_map/ppermute | solution.py:30
  56.2 11.4 %collective-permute-start.11 = (bf16[4,128,256]{2,1,0:T(8,128)(2,1)S(1)}, bf16[4,128,256]{2,1,0:T(8,128)(2,1)S(1)}, u32[]{:S(2)}, u32[]{:S(2)}) collective-permute-start(bf16[4,128,256]{2,1,0:T(8,128)(2,1)S(1)} %get-tuple-element.46), channel_id=1, source_target_pairs={{0,64},{1,65},{2,66},{3,67},{4,68},{5,69},{6,70},{7,71},{8,72},{9,... | collective-permute-start | bytes 786440 | tf_op jit(solution)/shard_map/ppermute | solution.py:30
  59.3 8.3 %collective-permute-start.12 = (bf16[4,128,256]{2,1,0:T(8,128)(2,1)S(1)}, bf16[4,128,256]{2,1,0:T(8,128)(2,1)S(1)}, u32[]{:S(2)}, u32[]{:S(2)}) collective-permute-start(bf16[4,128,256]{2,1,0:T(8,128)(2,1)S(1)} %get-tuple-element.47), channel_id=1, source_target_pairs={{0,32},{1,33},{2,34},{3,35},{4,36},{5,37},{6,38},{7,39},{8,40},{9,... | collective-permute-start | bytes 786440 | tf_op jit(solution)/shard_map/ppermute | solution.py:30
  59.9 7.8 %collective-permute-start.13 = (bf16[4,128,256]{2,1,0:T(8,128)(2,1)S(1)}, bf16[4,128,256]{2,1,0:T(8,128)(2,1)S(1)}, u32[]{:S(2)}, u32[]{:S(2)}) collective-permute-start(bf16[4,128,256]{2,1,0:T(8,128)(2,1)S(1)} %get-tuple-element.48), channel_id=1, source_target_pairs={{0,96},{1,97},{2,98},{3,99},{4,100},{5,101},{6,102},{7,103},{8,104... | collective-permute-start | bytes 786440 | tf_op jit(solution)/shard_map/ppermute | solution.py:30
  62.5 7.9 %copy-start.7 = (s32[16,1]{0,1:T(1,128)S(1)}, s32[16,1]{0,1:T(1,128)}, u32[]{:S(2)}) copy-start(s32[16,1]{0,1:T(1,128)} %param.10) | copy-start | bytes 196
  66.5 16.3 %collective-permute-start.18 = (bf16[128,1920]{1,0:T(8,128)(2,1)S(1)}, bf16[128,1920]{1,0:T(8,128)(2,1)S(1)}, u32[]{:S(2)}, u32[]{:S(2)}) collective-permute-start(bf16[128,1920]{1,0:T(8,128)(2,1)S(1)} %get-tuple-element.58), channel_id=1, source_target_pairs={{0,8},{1,9},{2,10},{3,11},{4,12},{5,13},{6,14},{7,15},{8,0},{9,1},... | collective-permute-start | bytes 1474568 | tf_op jit(solution)/shard_map/ppermute | solution.py:30
  68.5 5.6 %collective-permute-start.15 = (bf16[128,256]{1,0:T(8,128)(2,1)S(1)}, bf16[128,256]{1,0:T(8,128)(2,1)S(1)}, u32[]{:S(2)}, u32[]{:S(2)}) collective-permute-start(bf16[128,256]{1,0:T(8,128)(2,1)S(1)} %get-tuple-element.50), channel_id=1, source_target_pairs={{16,3},{17,0},{18,17},{19,18},{20,7},{21,4},{22,21},{23,22},{24,11... | collective-permute-start | bytes 196616 | tf_op jit(solution)/shard_map/ppermute | solution.py:30
  69.8 9.8 %collective-permute-start.17 = (bf16[128,256]{1,0:T(8,128)(2,1)S(1)}, bf16[128,256]{1,0:T(8,128)(2,1)S(1)}, u32[]{:S(2)}, u32[]{:S(2)}) collective-permute-start(bf16[128,256]{1,0:T(8,128)(2,1)S(1)} %get-tuple-element.52), channel_id=1, source_target_pairs={{16,1},{17,2},{18,19},{19,16},{20,5},{21,6},{22,23},{23,20},{24,9}... | collective-permute-start | bytes 196616 | tf_op jit(solution)/shard_map/ppermute | solution.py:30
  70.6 16.6 %collective-permute-start.19 = (bf16[128,1920]{1,0:T(8,128)(2,1)S(1)}, bf16[128,1920]{1,0:T(8,128)(2,1)S(1)}, u32[]{:S(2)}, u32[]{:S(2)}) collective-permute-start(bf16[128,1920]{1,0:T(8,128)(2,1)S(1)} %get-tuple-element.59), channel_id=1, source_target_pairs={{0,4},{1,5},{2,6},{3,7},{4,8},{5,9},{6,10},{7,11},{8,12},{9,13},{1... | collective-permute-start | bytes 1474568 | tf_op jit(solution)/shard_map/ppermute | solution.py:30
  71.7 15.5 %collective-permute-start.20 = (bf16[128,1920]{1,0:T(8,128)(2,1)S(1)}, bf16[128,1920]{1,0:T(8,128)(2,1)S(1)}, u32[]{:S(2)}, u32[]{:S(2)}) collective-permute-start(bf16[128,1920]{1,0:T(8,128)(2,1)S(1)} %get-tuple-element.60), channel_id=1, source_target_pairs={{0,12},{1,13},{2,14},{3,15},{4,0},{5,1},{6,2},{7,3},{8,4},{9,5},{1... | collective-permute-start | bytes 1474568 | tf_op jit(solution)/shard_map/ppermute | solution.py:30
  74.0 6.4 %collective-permute-start.14 = (bf16[128,512]{1,0:T(8,128)(2,1)S(1)}, bf16[128,512]{1,0:T(8,128)(2,1)S(1)}, u32[]{:S(2)}, u32[]{:S(2)}) collective-permute-start(bf16[128,512]{1,0:T(8,128)(2,1)S(1)} %get-tuple-element.49), channel_id=1, source_target_pairs={{0,16},{1,17},{2,2},{3,3},{4,48},{5,49},{6,34},{7,35},{8,80},{9,81... | collective-permute-start | bytes 393224 | tf_op jit(solution)/shard_map/ppermute | solution.py:30
  79.5 2.2 %collective-permute-start.16 = (bf16[128,512]{1,0:T(8,128)(2,1)S(1)}, bf16[128,512]{1,0:T(8,128)(2,1)S(1)}, u32[]{:S(2)}, u32[]{:S(2)}) collective-permute-start(bf16[128,512]{1,0:T(8,128)(2,1)S(1)} %get-tuple-element.51), channel_id=1, source_target_pairs={{0,0},{1,1},{2,18},{3,19},{4,32},{5,33},{6,50},{7,51},{8,64},{9,65... | collective-permute-start | bytes 393224 | tf_op jit(solution)/shard_map/ppermute | solution.py:30
  80.5 24.0 %collective-permute-start.21 = (bf16[1920,256]{1,0:T(8,128)(2,1)}, bf16[1920,256]{1,0:T(8,128)(2,1)}, u32[]{:S(2)}, u32[]{:S(2)}) collective-permute-start(bf16[1920,256]{1,0:T(8,128)(2,1)} %get-tuple-element.62), channel_id=1, source_target_pairs={{0,2},{1,3},{2,0},{3,1},{4,6},{5,7},{6,4},{7,5},{8,10},{9,11},{10,... | collective-permute-start | bytes 2949128 | tf_op jit(solution)/shard_map/ppermute | solution.py:30
  81.7 30.7 %collective-permute-start.22 = (bf16[1920,256]{1,0:T(8,128)(2,1)}, bf16[1920,256]{1,0:T(8,128)(2,1)}, u32[]{:S(2)}, u32[]{:S(2)}) collective-permute-start(bf16[1920,256]{1,0:T(8,128)(2,1)} %get-tuple-element.63), channel_id=1, source_target_pairs={{0,1},{1,2},{2,3},{3,0},{4,5},{5,6},{6,7},{7,4},{8,9},{9,10},{10,1... | collective-permute-start | bytes 2949128 | tf_op jit(solution)/shard_map/ppermute | solution.py:30
  82.8 29.5 %collective-permute-start.23 = (bf16[1920,256]{1,0:T(8,128)(2,1)}, bf16[1920,256]{1,0:T(8,128)(2,1)}, u32[]{:S(2)}, u32[]{:S(2)}) collective-permute-start(bf16[1920,256]{1,0:T(8,128)(2,1)} %get-tuple-element.64), channel_id=1, source_target_pairs={{0,3},{1,0},{2,1},{3,2},{4,7},{5,4},{6,5},{7,6},{8,11},{9,8},{10,9... | collective-permute-start | bytes 2949128 | tf_op jit(solution)/shard_map/ppermute | solution.py:30
  89.4 23.0 %copy-start.4 = (bf16[1920,256]{1,0:T(8,128)(2,1)S(1)}, bf16[1920,256]{1,0:T(8,128)(2,1)}, u32[]{:S(2)}) copy-start(bf16[1920,256]{1,0:T(8,128)(2,1)} %copy-done.3) | copy-start | bytes 2949124
  89.4 37.7 %all-to-all-start = ((bf16[16,16,2432]{2,1,0:T(8,128)(2,1)}), bf16[16,16,2432]{2,1,0:T(8,128)(2,1)S(1)}, u32[]{:S(2)}, u32[]{:S(2)}) async-start(bf16[16,16,2432]{2,1,0:T(8,128)(2,1)} %bitcast.8), calls=%async_computation | async-start | bytes 2490368 | tf_op jit(solution)/shard_map/all_to_all | solution.py:305
